TPU v7x, 32 devices: a whole 2x2x4 slice. The times are simulated.
32 devices in a mesh: doc: 4 (over z), feat: 8 (over y, x, core).
Axes of the slice: x: 2, y: 2, z: 4, core: 2. Of those that a mesh axis runs over, the one named last changes fastest.
Arguments:
- documents: bfloat16 [512, 512], P('doc', 'feat'), may hold values from -6 to 6
- directions: bfloat16 [512, 32768], P('doc', 'feat'), may hold values from -0.5 to 0.5
- phase: float32 [32768], P('feat'), may hold values from -3.140625 to 3.140625
- amplitude: float32 [32768], P('feat'), may hold values from 0.4 to 2.3
- doc_weight: float32 [512], P('doc'), may hold values from 0.5 to 4.2
- labels: int32 [512], P('doc'), may hold values from 0 to 127
Outputs:
- margins: float32 [512, 128], P('doc')
- scaled_weights: float32 [32768, 128], P('feat')
All inputs are finite; a program needn't handle non-finite values.
Results may differ from a plain program's by a relative error of at most 0.0003.
Values may be sent and summed in bfloat16 or wider, within the bound.
A program may use at most 64 MiB of HBM per device.

v0:
```python
import jax
import jax.numpy as jnp
from jax import lax
from jax.sharding import PartitionSpec as P

C = 128
ITERS = 3
NEWTON = 3
shrink_level = 0.1
ratio_floor = 1e-06


def project_tile(features, factor, start, target):
    residue = target - jnp.dot(features, start, precision=lax.Precision.HIGHEST)
    halfway = lax.linalg.triangular_solve(factor, residue, left_side=True, lower=True)
    solved = lax.linalg.triangular_solve(
        factor, halfway, left_side=True, lower=True, transpose_a=True
    )
    new_copy = start + lax.dot_general(
        features, solved, (((0,), (0,)), ((), ())), precision=lax.Precision.HIGHEST
    )
    new_part = jnp.dot(features, new_copy, precision=lax.Precision.HIGHEST)
    return (new_copy, new_part)


def logistic_prox(target, signs, weight_ratio):
    current = target
    for newton_step in range(NEWTON):
        chance = jax.nn.sigmoid(-signs * current)
        gradient = current - target - weight_ratio * signs * chance
        current = current - gradient / (1.0 + weight_ratio * chance * (1.0 - chance))
    return current


def shrink_values(target, limit):
    return target - jnp.clip(target, -limit, limit)


def per_device(documents, directions, phase, amplitude, doc_weight, labels):
    doc_full = lax.all_gather(documents, "feat", axis=1, tiled=True)
    doc_count = documents.shape[0]
    width_tile = directions.shape[1]
    num_feat = lax.axis_size("feat")
    num_doc = lax.axis_size("doc")
    angles = jnp.dot(
        doc_full,
        lax.all_gather(directions, "doc", axis=0, tiled=True),
        preferred_element_type=jnp.float32,
    )
    features = jnp.sqrt(2.0 / width_tile) * amplitude * jnp.cos(angles + phase)
    gram = jnp.eye(doc_count, dtype=jnp.float32) + lax.dot_general(
        features, features, (((1,), (1,)), ((), ())), precision=lax.Precision.HIGHEST
    )
    factor = jnp.linalg.cholesky(gram)
    signs = jnp.where(labels[:, None] == jnp.arange(C, dtype=jnp.int32)[None, :], 1.0, -1.0).astype(
        jnp.float32
    )
    share_rows = doc_count // num_feat
    offset = lax.axis_index("feat") * share_rows
    local_signs = lax.dynamic_slice_in_dim(signs, offset, share_rows, 0)
    local_weight = lax.dynamic_slice_in_dim(doc_weight, offset, share_rows, 0)[:, None]
    rho = jnp.float32(1.0)
    margins = logistic_prox(
        jnp.zeros(local_signs.shape, jnp.float32), local_signs, local_weight / rho
    )
    sums = jnp.zeros(local_signs.shape, jnp.float32)
    duals_y = jnp.zeros(local_signs.shape, jnp.float32)
    duals_x = jnp.zeros((width_tile, C), jnp.float32)
    partial_value = jnp.zeros((doc_count, C), jnp.float32)
    weights = jnp.zeros((width_tile, C), jnp.float32)
    for step in range(ITERS):
        correction = (margins - duals_y - sums) / num_feat
        correction = lax.all_gather(correction, "feat", axis=0, tiled=True)
        new_copy, partial_value = project_tile(
            features, factor, weights - duals_x, partial_value + correction
        )
        sums = lax.psum_scatter(partial_value, "feat", scatter_dimension=0, tiled=True)
        old_weights = weights
        old_margins = margins
        limit = shrink_level / (rho * num_doc)
        summed = lax.psum(new_copy + duals_x, "doc")
        weights = shrink_values(summed / num_doc, limit)
        margins = logistic_prox(sums + duals_y, local_signs, local_weight / rho)
        duals_x = duals_x + new_copy - weights
        duals_y = duals_y + sums - margins
        if step + 1 < ITERS:
            margin_gap = jnp.sum((sums - margins) ** 2)
            margin_move = jnp.sum((margins - old_margins) ** 2)
            primal, dual_norm = lax.psum(
                (
                    jnp.sum((new_copy - weights) ** 2) + margin_gap,
                    jnp.sum((weights - old_weights) ** 2) + margin_move,
                ),
                ("doc", "feat"),
            )
            dual_norm = rho * rho * dual_norm
            growth = ((primal + ratio_floor) / (dual_norm + ratio_floor)) ** 0.25
            rho = rho * growth
            duals_x = duals_x / growth
            duals_y = duals_y / growth
    margins = lax.all_gather(margins, "feat", axis=0, tiled=True)
    return (margins, num_feat * weights)


def solution(mesh):
    in_specs = (P("doc", "feat"), P("doc", "feat"), P("feat"), P("feat"), P("doc"), P("doc"))
    out_specs = (P("doc", None), P("feat", None))
    return jax.shard_map(
        per_device, mesh=mesh, in_specs=in_specs, out_specs=out_specs, check_vma=False
    )
```

profile of v0, /device:TPU:0, one launch (start us, length us, event | category | flops | bytes accessed | tf_op | source)
XLA Modules:
  0.0 668.8 jit_solution(7295771002411407596)
XLA Ops:
  7.2 0.0 all-gather.2.cloned.1.call-start
  7.2 0.7 all-gather.2.cloned.1.call-update
  7.9 0.0 reduce-scatter.4.cloned.1.call-start
  7.9 0.7 dynamic-slice
  8.7 0.7 dynamic_slice.6
  9.4 0.1 broadcast_multiply_fusion.1
  9.6 10.7 %all_gather.20 = f32[128,128]{1,0:T(8,128)S(1)} all-gather(f32[16,128]{1,0:T(8,128)S(1)} %broadcast_multiply_fusion.1), channel_id=1, replica_groups=mesh['doc'=4,'feat'=8] {'feat'}, dimensions={0}, use_global_device_ids=true | all-gather | bytes 73728 | tf_op jit(solution)/shard_map/all_gather | solution.py:73
  20.3 9.2 %all_gather.18 = bf16[128,512]{0,1:T(8,128)(2,1)S(1)} all-gather(bf16[128,64]{0,1:T(8,128)(2,1)} %param.10), channel_id=1, replica_groups=mesh['doc'=4,'feat'=8] {'feat'}, dimensions={1}, use_global_device_ids=true | all-gather | bytes 147456 | tf_op jit(solution)/shard_map/all_gather | solution.py:40
  29.5 0.7 broadcast_multiply_fusion
  30.2 62.9 %all-gather.2.cloned.1.call-done = bf16[512,4096]{1,0:T(8,128)(2,1)} async-done(((bf16[128,4096]{1,0:T(8,128)(2,1)}), bf16[512,4096]{1,0:T(8,128)(2,1)}) %all-gather.2.cloned.1.call-update) | async-done | bytes 4194320 | tf_op jit(solution)/shard_map/all_gather | solution.py:47
  93.0 9.5 %fusion.1 = f32[128,4096]{1,0:T(8,128)S(1)} fusion(bf16[128,512]{0,1:T(8,128)(2,1)S(1)} %all_gather.18, bf16[512,4096]{1,0:T(8,128)(2,1)} %all-gather.2.cloned.1.call-done, f32[4096]{0:T(1024)} %param.12, f32[4096]{0:T(1024)S(1)} %broadcast_multiply_fusion), kind=kOutput, calls=%fused_computation.4 | convolution fusion | flops 537919488 | bytes 6455296 | tf_op jit(solution)/shard_map/dot_general | solution.py:45
  102.5 1.8 fusion.140
  104.3 1.8 convolution_subtract_fusion.2
  106.1 0.1 copy.8
  106.2 11.7 %cholesky.20 = f32[128,128]{1,0:T(8,128)S(1)} custom-call(f32[128,128]{1,0:T(8,128)S(1)} %fusion.22), custom_call_target="Cholesky" | custom-call | tf_op jit(solution)/shard_map/jit(cholesky)/cholesky | solution.py:54
  118.0 0.6 compare_reduce_fusion
  118.6 0.7 fusion.8
  119.3 9.8 %custom-call.14 = f32[1,128,128]{1,2,0:T(8,128)S(1)} custom-call(f32[1,128,128]{2,1,0:T(8,128)S(1)} %fusion.8), custom_call_target="InvertDiagBlocksLowerTriangular" | custom-call | tf_op jit(solution)/shard_map/triangular_solve/custom-call.2 | solution.py:16
  129.1 0.3 fusion.17
  129.4 0.2 fusion.19
  129.6 16.5 %fusion.141 = f32[4096,128]{1,0:T(8,128)} fusion(f32[128,4096]{1,0:T(8,128)S(1)} %fusion.1, f32[128,128]{1,0:T(8,128)S(1)} %fusion.19), kind=kOutput, calls=%fused_computation.176 | convolution fusion | flops 805306368 | bytes 4259840 | tf_op jit(solution)/shard_map/dot_general | solution.py:19
  146.1 4.4 fusion.142
  150.4 0.0 reduce-scatter.4.cloned.1.call-update
  150.5 0.0 all-reduce.6.cloned.1.call-start
  150.5 0.7 all-reduce.6.cloned.1.call-update
  151.2 0.0 reduce-scatter.6.cloned.1.call-start
  151.2 31.4 %reduce-scatter.4.cloned.1.call-done = f32[16,128]{1,0:T(8,128)} async-done(((f32[128,128]{1,0:T(8,128)}), f32[16,128]{1,0:T(8,128)}) %reduce-scatter.4.cloned.1.call-update) | async-done | bytes 8208 | tf_op jit(solution)/shard_map/reduce_scatter | solution.py:77
  182.6 1.5 multiply_reduce_fusion.6
  184.1 1.4 multiply_reduce_fusion.7
  185.5 86.3 %all-reduce.6.cloned.1.call-done = f32[4096,128]{1,0:T(8,128)} async-done(((f32[4096,128]{1,0:T(8,128)}), f32[4096,128]{1,0:T(8,128)}) %all-reduce.6.cloned.1.call-update) | async-done | bytes 2097168 | tf_op jit(solution)/shard_map/psum | solution.py:81
  271.8 3.4 multiply_reduce_fusion.2
  277.5 39.3 %all-reduce.1 = (f32[]{:T(128)}, f32[]{:T(128)}) all-reduce(f32[]{:T(128)S(6)} %add.189, f32[]{:T(128)S(6)} %add.191), channel_id=1, replica_groups=mesh['doc'=4,'feat'=8] {'doc','feat'}, use_global_device_ids=true, to_apply=%region_6.9 | all-reduce | flops 2 | bytes 16 | tf_op jit(solution)/shard_map/psum | solution.py:89
  318.2 10.2 %all_gather.21 = f32[128,128]{1,0:T(8,128)S(1)} all-gather(f32[16,128]{1,0:T(8,128)S(1)} %subtract_multiply_fusion.2), channel_id=1, replica_groups=mesh['doc'=4,'feat'=8] {'feat'}, dimensions={0}, use_global_device_ids=true | all-gather | bytes 73728 | tf_op jit(solution)/shard_map/all_gather | solution.py:73
  328.4 4.9 convolution_subtract_fusion.1
  333.3 0.3 fusion.13
  333.6 0.2 fusion.15
  333.8 5.1 fusion.5
  338.9 1.3 copy-done.2
  340.2 2.8 fusion.143
  343.0 0.0 reduce-scatter.6.cloned.1.call-update
  343.0 0.0 all-reduce.8.cloned.1.call-start
  343.1 0.5 all-reduce.8.cloned.1.call-update
  343.6 0.0 reduce-scatter.8.cloned.1.call-start
  343.7 0.1 broadcast_divide_fusion.3
  343.8 31.9 %reduce-scatter.6.cloned.1.call-done = f32[16,128]{1,0:T(8,128)} async-done(((f32[128,128]{1,0:T(8,128)}), f32[16,128]{1,0:T(8,128)}) %reduce-scatter.6.cloned.1.call-update) | async-done | bytes 8208 | tf_op jit(solution)/shard_map/reduce_scatter | solution.py:77
  375.7 1.5 multiply_reduce_fusion.4
  377.2 87.4 %all-reduce.8.cloned.1.call-done = f32[4096,128]{1,0:T(8,128)} async-done(((f32[4096,128]{1,0:T(8,128)}), f32[4096,128]{1,0:T(8,128)}) %all-reduce.8.cloned.1.call-update) | async-done | bytes 2097168 | tf_op jit(solution)/shard_map/psum | solution.py:81
  464.7 4.4 multiply_reduce_fusion
  471.5 39.3 %all-reduce = (f32[]{:T(128)}, f32[]{:T(128)}) all-reduce(f32[]{:T(128)S(6)} %add.203, f32[]{:T(128)S(6)} %add.205), channel_id=1, replica_groups=mesh['doc'=4,'feat'=8] {'doc','feat'}, use_global_device_ids=true, to_apply=%region_14.17 | all-reduce | flops 2 | bytes 16 | tf_op jit(solution)/shard_map/psum | solution.py:89
  512.2 10.5 %all_gather.22 = f32[128,128]{1,0:T(8,128)S(1)} all-gather(f32[16,128]{1,0:T(8,128)S(1)} %subtract_multiply_fusion.1), channel_id=1, replica_groups=mesh['doc'=4,'feat'=8] {'feat'}, dimensions={0}, use_global_device_ids=true | all-gather | bytes 73728 | tf_op jit(solution)/shard_map/all_gather | solution.py:73
  522.7 5.0 convolution_subtract_fusion
  527.7 0.3 fusion.9
  527.9 0.2 fusion.11
  528.2 5.1 fusion.6
  533.3 2.8 fusion.144
  536.1 0.0 all-reduce.10.cloned.1.call-start
  536.1 0.7 all-reduce.10.cloned.1.call-update
  536.9 0.1 broadcast_divide_fusion.2
  537.0 31.8 %reduce-scatter.8.cloned.1.call-done = f32[16,128]{1,0:T(8,128)} async-done(((f32[128,128]{1,0:T(8,128)}), f32[16,128]{1,0:T(8,128)}) %reduce-scatter.8.cloned.1.call-update) | async-done | bytes 8208 | tf_op jit(solution)/shard_map/reduce_scatter | solution.py:77
  568.8 0.8 fusion.64
  569.6 9.2 %all_gather.23 = f32[128,128]{1,0:T(8,128)S(1)} all-gather(f32[16,128]{1,0:T(8,128)S(1)} %fusion.64), channel_id=1, replica_groups=mesh['doc'=4,'feat'=8] {'feat'}, dimensions={0}, use_global_device_ids=true | all-gather | bytes 73728 | tf_op jit(solution)/shard_map/all_gather | solution.py:101
  578.8 79.0 %all-reduce.10.cloned.1.call-done = f32[4096,128]{1,0:T(8,128)} async-done(((f32[4096,128]{1,0:T(8,128)}), f32[4096,128]{1,0:T(8,128)}) %all-reduce.10.cloned.1.call-update) | async-done | bytes 2097168 | tf_op jit(solution)/shard_map/psum | solution.py:81
  657.9 3.2 subtract_multiply_fusion
  661.1 0.6 copy.13
  (24 shorter events, 0.1 us)
Async XLA Ops:
  7.2 85.9 %all-gather.2.cloned.1.call-start = ((), (), s32[]{:S(2)}) async-start(), calls=%async_computation.3 | async-start | bytes 5242880 | tf_op jit(solution)/shard_map/all_gather | solution.py:47
  7.9 174.7 %reduce-scatter.4.cloned.1.call-start = ((), (), s32[]{:S(2)}) async-start(), calls=%async_computation.5 | async-start | bytes 73728 | tf_op jit(solution)/shard_map/reduce_scatter | solution.py:77
  150.5 121.3 %all-reduce.6.cloned.1.call-start = ((), (), s32[]{:S(2)}) async-start(), calls=%async_computation.4 | async-start | bytes 4194304 | tf_op jit(solution)/shard_map/psum | solution.py:81
  151.2 224.5 %reduce-scatter.6.cloned.1.call-start = ((), (), s32[]{:S(2)}) async-start(), calls=%async_computation.7 | async-start | bytes 73728 | tf_op jit(solution)/shard_map/reduce_scatter | solution.py:77
  185.5 132.7 %copy-start.8 = (f32[16,128]{1,0:T(8,128)S(1)}, f32[16,128]{1,0:T(8,128)}, u32[]{:S(2)}) copy-start(f32[16,128]{1,0:T(8,128)} %reduce-scatter.4.cloned.1.call-done) | copy-start | bytes 24580
  185.5 142.9 %copy-start.6 = (f32[128,128]{1,0:T(8,128)S(1)}, f32[128,128]{1,0:T(8,128)}, u32[]{:S(2)}) copy-start(f32[128,128]{1,0:T(8,128)} %fusion.142) | copy-start | bytes 196612
  328.4 5.4 copy-start
  328.4 5.4 copy-start.1
  338.9 1.3 copy-start.2
  343.0 0.7 copy-start.9
  343.0 121.6 %all-reduce.8.cloned.1.call-start = ((), (), s32[]{:S(2)}) async-start(), calls=%async_computation.6 | async-start | bytes 4194304 | tf_op jit(solution)/shard_map/psum | solution.py:81
  343.6 225.2 %reduce-scatter.8.cloned.1.call-start = ((), (), s32[]{:S(2)}) async-start(), calls=%async_computation.8 | async-start | bytes 73728 | tf_op jit(solution)/shard_map/reduce_scatter | solution.py:77
  377.2 135.0 %copy-start.7 = (f32[16,128]{1,0:T(8,128)S(1)}, f32[16,128]{1,0:T(8,128)}, u32[]{:S(2)}) copy-start(f32[16,128]{1,0:T(8,128)} %reduce-scatter.6.cloned.1.call-done) | copy-start | bytes 24580
  377.2 145.4 %copy-start.5 = (f32[128,128]{1,0:T(8,128)S(1)}, f32[128,128]{1,0:T(8,128)}, u32[]{:S(2)}) copy-start(f32[128,128]{1,0:T(8,128)} %fusion.143) | copy-start | bytes 196612
  522.7 5.5 copy-start.3
  522.7 5.5 copy-start.4
  536.1 121.8 %all-reduce.10.cloned.1.call-start = ((), (), s32[]{:S(2)}) async-start(), calls=%async_computation.9 | async-start | bytes 4194304 | tf_op jit(solution)/shard_map/psum | solution.py:81
Sparse Core Ops, SparseCore 0:
  9.5 83.4 all-gather.1
  150.6 32.0 reduce-scatter.3
  185.6 86.1 all-reduce.5
  343.2 32.5 reduce-scatter.5
  378.5 86.0 all-reduce.7
  536.2 32.5 reduce-scatter.7
  571.7 86.0 all-reduce.9
where the time goes:
time: 673 us; the launch traced here: 669 us
  waiting for transfers between devices  413 us (61%)
  blocking collectives  128 us (19%)
  matrix products  61 us (9%)
  other arithmetic  40.1 us (6%)
  between operations  22.2 us (3%)
    psum x3, waiting for transfers between devices, per_device(): summed = lax.psum(new_copy + duals_x, 'doc')  253 us
    reduce_scatter x3, waiting for transfers between devices, per_device(): lax.psum_scatter(partial_value, 'feat', scatter_dimension=0, tiled=True)  95.1 us
    psum x2, blocking collectives, per_device(): lax.psum((jnp.sum((new_copy - weights) ** 2) + margin_gap, jnp.sum((weigh...  78.6 us
    all_gather x1, waiting for transfers between devices, per_device(): lax.all_gather(directions, 'doc', axis=0, tiled=True)  62.9 us
    all_gather x3, blocking collectives, per_device(): correction = lax.all_gather(correction, 'feat', axis=0, tiled=True)  31.4 us
    dot_general x3, matrix products, project_tile(): lax.dot_general(features, solved, (((0,), (0,)), ((), ())), precision=lax...  26.6 us
  transfers between devices with their start and end apart: 7, of which 7 were waited for; matrix products, arithmetic and copies ran while one was open for 1% of the time, Pallas kernels for 0%

commit v1 on v0

--- a/solution.py
+++ b/solution.py
@@ -8,6 +8,22 @@
 NEWTON = 3
 shrink_level = 0.1
 ratio_floor = 1e-06
+
+
+def columns_settle(state):
+    left_arr = lax.axis_index("doc")
+    view_out = lax.axis_size("doc")
+    low, earlier, piece_now = (view_out, left_arr, state.shape[0])
+    ready = jnp.zeros([q * low if p == 0 else q for p, q in enumerate(state.shape)], state.dtype)
+    placed = lax.dynamic_update_slice_in_dim(ready, state, earlier * piece_now, axis=0)
+    k0 = 1
+    while k0 < low:
+        state = lax.ppermute(state, "doc", [(p, (p + 1) % low) for p in range(low)])
+        placed = lax.dynamic_update_slice_in_dim(
+            placed, state, (earlier - k0) % low * piece_now, axis=0
+        )
+        k0 += 1
+    return placed
 
 
 def project_tile(features, factor, start, target):
@@ -42,11 +58,7 @@
     width_tile = directions.shape[1]
     num_feat = lax.axis_size("feat")
     num_doc = lax.axis_size("doc")
-    angles = jnp.dot(
-        doc_full,
-        lax.all_gather(directions, "doc", axis=0, tiled=True),
-        preferred_element_type=jnp.float32,
-    )
+    angles = jnp.dot(doc_full, columns_settle(directions), preferred_element_type=jnp.float32)
     features = jnp.sqrt(2.0 / width_tile) * amplitude * jnp.cos(angles + phase)
     gram = jnp.eye(doc_count, dtype=jnp.float32) + lax.dot_general(
         features, features, (((1,), (1,)), ((), ())), precision=lax.Precision.HIGHEST

time: 673 us -> 563 us (0.84)
  waiting for transfers between devices: 413 us -> 300 us
    psum x3, waiting for transfers between devices: 253 us -> 153 us  [per_device(): summed = lax.psum(new_copy + duals_x, 'doc')]
    all_gather x1 -> x0, waiting for transfers between devices: 62.9 us -> none  [per_device(): lax.all_gather(directions, 'doc', axis=0, tiled=True)]
    ppermute x0 -> x3, waiting for transfers between devices: none -> 50.6 us  [columns_settle(): state = lax.ppermute(state, 'doc', [(p, (p + 1) % low) for p in range(low)])]
    dot_general x3, matrix products: 26.6 us -> 10.1 us  [project_tile(): lax.dot_general(features, solved, (((0,), (0,)), ((), ())), precision=lax...]
  transfers between devices with their start and end apart: 7 -> 9, of which waited for: 7 -> 9; matrix products, arithmetic and copies ran while one was open for 1% -> 2% of each run, Pallas kernels for 0% -> 0%
where the time goes in v1:
time: 563 us; the launch traced here: 559 us
  waiting for transfers between devices  300 us (53%)
  blocking collectives  127 us (23%)
  matrix products  55 us (10%)
  other arithmetic  40.3 us (7%)
  between operations  23.5 us (4%)
  local copies, waits for them, and re-layouts  10.2 us (2%)
    psum x3, waiting for transfers between devices, per_device(): summed = lax.psum(new_copy + duals_x, 'doc')  153 us
    reduce_scatter x3, waiting for transfers between devices, per_device(): lax.psum_scatter(partial_value, 'feat', scatter_dimension=0, tiled=True)  94.7 us
    psum x2, blocking collectives, per_device(): lax.psum((jnp.sum((new_copy - weights) ** 2) + margin_gap, jnp.sum((weigh...  78.8 us
    ppermute x3, waiting for transfers between devices, columns_settle(): state = lax.ppermute(state, 'doc', [(p, (p + 1) % low) for p in range(low)])  50.6 us
    all_gather x3, blocking collectives, per_device(): correction = lax.all_gather(correction, 'feat', axis=0, tiled=True)  30 us
    dot_general x3, matrix products, project_tile(): residue = target - jnp.dot(features, start, precision=lax.Precision.HIGHEST)  15.8 us
    dot_general x3, matrix products, project_tile(): new_part = jnp.dot(features, new_copy, precision=lax.Precision.HIGHEST)  13.9 us
    another operation x3, other arithmetic, per_device(): factor = jnp.linalg.cholesky(gram)  12.4 us
  transfers between devices with their start and end apart: 9, of which 9 were waited for; matrix products, arithmetic and copies ran while one was open for 2% of the time, Pallas kernels for 0%

profile of v1, /device:TPU:0, one launch (start us, length us, event | category | flops | bytes accessed | tf_op | source)
XLA Modules:
  0.0 559.2 jit_solution(318528297586975134)
XLA Ops:
  8.0 3.1 collective-permute-start
  11.1 25.4 %collective-permute-done = bf16[128,4096]{1,0:T(8,128)(2,1)S(1)} collective-permute-done((bf16[128,4096]{1,0:T(8,128)(2,1)}, bf16[128,4096]{1,0:T(8,128)(2,1)S(1)}, u32[]{:S(2)}, u32[]{:S(2)}) %collective-permute-start) | collective-permute-done | bytes 1048608 | tf_op jit(solution)/shard_map/ppermute | solution.py:21
  36.5 0.7 dynamic-slice
  37.3 0.7 dynamic_slice.6
  38.0 0.7 broadcast_multiply_fusion
  38.7 2.4 broadcast_in_dim.18
  41.2 1.1 constant_dynamic-update-slice_fusion.3
  42.2 20.4 %collective-permute-done.1 = bf16[128,4096]{1,0:T(8,128)(2,1)S(1)} collective-permute-done((bf16[128,4096]{1,0:T(8,128)(2,1)S(1)}, bf16[128,4096]{1,0:T(8,128)(2,1)S(1)}, u32[]{:S(2)}, u32[]{:S(2)}) %collective-permute-start.1) | collective-permute-done | bytes 1048608 | tf_op jit(solution)/shard_map/ppermute | solution.py:21
  62.7 0.1 broadcast_multiply_fusion.1
  62.9 9.0 %all_gather.16 = f32[128,128]{1,0:T(8,128)S(1)} all-gather(f32[16,128]{1,0:T(8,128)S(1)} %broadcast_multiply_fusion.1), channel_id=1, replica_groups=mesh['doc'=4,'feat'=8] {'feat'}, dimensions={0}, use_global_device_ids=true | all-gather | bytes 73728 | tf_op jit(solution)/shard_map/all_gather | solution.py:85
  71.9 9.2 %all_gather.15 = bf16[128,512]{0,1:T(8,128)(2,1)S(1)} all-gather(bf16[128,64]{0,1:T(8,128)(2,1)S(1)} %copy-done.11), channel_id=1, replica_groups=mesh['doc'=4,'feat'=8] {'feat'}, dimensions={1}, use_global_device_ids=true | all-gather | bytes 147456 | tf_op jit(solution)/shard_map/all_gather | solution.py:56
  81.1 1.0 constant_dynamic-update-slice_fusion.2
  82.1 1.1 constant_dynamic-update-slice_fusion.1
  83.2 4.7 collective-permute-done.2
  87.9 1.1 constant_dynamic-update-slice_fusion
  89.0 10.2 %fusion.1 = f32[4096,128]{1,0:T(8,128)S(1)} fusion(bf16[512,4096]{1,0:T(8,128)(2,1)} %constant_dynamic-update-slice_fusion, bf16[128,512]{0,1:T(8,128)(2,1)S(1)} %all_gather.15, f32[4096]{0:T(1024)S(1)} %copy-done.8, f32[4096]{0:T(1024)S(1)} %broadcast_multiply_fusion), kind=kOutput, calls=%fused_computation.4 | convolution fusion | flops 537919488 | bytes 6455296 | tf_op jit(solution)/shard_map/dot_general | solution.py:61
  99.3 3.5 fusion.140
  102.7 3.4 convolution_subtract_fusion.2
  106.2 0.1 copy.8
  106.3 11.7 %cholesky.20 = f32[128,128]{1,0:T(8,128)S(1)} custom-call(f32[128,128]{1,0:T(8,128)S(1)} %fusion.22), custom_call_target="Cholesky" | custom-call | tf_op jit(solution)/shard_map/jit(cholesky)/cholesky | solution.py:66
  118.0 0.6 compare_reduce_fusion
  118.7 0.7 fusion.8
  119.3 10.0 %custom-call.14 = f32[1,128,128]{1,2,0:T(8,128)S(1)} custom-call(f32[1,128,128]{2,1,0:T(8,128)S(1)} %fusion.8), custom_call_target="InvertDiagBlocksLowerTriangular" | custom-call | tf_op jit(solution)/shard_map/triangular_solve/custom-call.2 | solution.py:32
  129.3 0.3 fusion.17
  129.6 0.2 fusion.19
  129.8 3.1 fusion.141
  133.0 5.7 %fusion.142 = f32[128,128]{1,0:T(8,128)} fusion(f32[4096,128]{1,0:T(8,128)S(1)} %fusion.1, f32[4096,128]{1,0:T(8,128)} %fusion.141), kind=kOutput, calls=%fused_computation.181 | convolution fusion | flops 805306368 | bytes 4259840 | tf_op jit(solution)/shard_map/dot_general | solution.py:38
  138.6 0.0 all-reduce.6.cloned.1.call-start
  138.7 0.5 all-reduce.6.cloned.1.call-update
  139.3 30.8 %reduce-scatter.4.cloned.1.call-done = f32[16,128]{1,0:T(8,128)} async-done(((f32[128,128]{1,0:T(8,128)}), f32[16,128]{1,0:T(8,128)}) %reduce-scatter.4.cloned.1.call-update) | async-done | bytes 8208 | tf_op jit(solution)/shard_map/reduce_scatter | solution.py:89
  170.1 1.5 multiply_reduce_fusion.6
  171.6 1.4 multiply_reduce_fusion.7
  172.9 52.9 %all-reduce.6.cloned.1.call-done = f32[4096,128]{1,0:T(8,128)} async-done(((f32[4096,128]{1,0:T(8,128)}), f32[4096,128]{1,0:T(8,128)}) %all-reduce.6.cloned.1.call-update) | async-done | bytes 2097168 | tf_op jit(solution)/shard_map/psum | solution.py:93
  225.8 3.4 multiply_reduce_fusion.2
  231.6 39.3 %all-reduce.1 = (f32[]{:T(128)}, f32[]{:T(128)}) all-reduce(f32[]{:T(128)S(6)} %add.222, f32[]{:T(128)S(6)} %add.224), channel_id=1, replica_groups=mesh['doc'=4,'feat'=8] {'doc','feat'}, use_global_device_ids=true, to_apply=%region_6.9 | all-reduce | flops 2 | bytes 16 | tf_op jit(solution)/shard_map/psum | solution.py:101
  272.2 10.6 %all_gather.17 = f32[128,128]{1,0:T(8,128)S(1)} all-gather(f32[16,128]{1,0:T(8,128)S(1)} %subtract_multiply_fusion.2), channel_id=1, replica_groups=mesh['doc'=4,'feat'=8] {'feat'}, dimensions={0}, use_global_device_ids=true | all-gather | bytes 73728 | tf_op jit(solution)/shard_map/all_gather | solution.py:85
  282.9 6.2 %convolution_subtract_fusion.1 = f32[128,128]{1,0:T(8,128)S(1)} fusion(f32[4096,128]{1,0:T(8,128)S(1)} %fusion.1, f32[128,128]{1,0:T(8,128)S(1)} %copy-done.7, f32[128,128]{1,0:T(8,128)S(1)} %all_gather.17, f32[4096,128]{1,0:T(8,128)} %all-reduce.6.cloned.1.call-done, f32[]{:T(128)S(6)} %pow.6, f32[4096,128]{1,0:T(8,128)} %fusion.141), kind=kOutput, calls=%fused_computation.14 | convolution fusion | flops 808484864 | bytes 6488068 | tf_op jit(solution)/shard_map/dot_general | solution.py:30
  289.1 0.3 fusion.13
  289.4 0.2 fusion.15
  289.6 3.5 fusion.5
  293.1 1.3 copy-done.2
  294.4 4.1 fusion.143
  298.6 0.5 all-reduce.8.cloned.1.call-update
  299.2 0.1 broadcast_divide_fusion.3
  299.3 31.9 %reduce-scatter.6.cloned.1.call-done = f32[16,128]{1,0:T(8,128)} async-done(((f32[128,128]{1,0:T(8,128)}), f32[16,128]{1,0:T(8,128)}) %reduce-scatter.6.cloned.1.call-update) | async-done | bytes 8208 | tf_op jit(solution)/shard_map/reduce_scatter | solution.py:89
  331.2 1.5 multiply_reduce_fusion.4
  332.7 54.2 %all-reduce.8.cloned.1.call-done = f32[4096,128]{1,0:T(8,128)} async-done(((f32[4096,128]{1,0:T(8,128)}), f32[4096,128]{1,0:T(8,128)}) %all-reduce.8.cloned.1.call-update) | async-done | bytes 2097168 | tf_op jit(solution)/shard_map/psum | solution.py:93
  386.9 4.4 multiply_reduce_fusion
  393.8 39.5 %all-reduce = (f32[]{:T(128)}, f32[]{:T(128)}) all-reduce(f32[]{:T(128)S(6)} %add.236, f32[]{:T(128)S(6)} %add.238), channel_id=1, replica_groups=mesh['doc'=4,'feat'=8] {'doc','feat'}, use_global_device_ids=true, to_apply=%region_14.17 | all-reduce | flops 2 | bytes 16 | tf_op jit(solution)/shard_map/psum | solution.py:101
  434.6 10.3 %all_gather.18 = f32[128,128]{1,0:T(8,128)S(1)} all-gather(f32[16,128]{1,0:T(8,128)S(1)} %subtract_multiply_fusion.1), channel_id=1, replica_groups=mesh['doc'=4,'feat'=8] {'feat'}, dimensions={0}, use_global_device_ids=true | all-gather | bytes 73728 | tf_op jit(solution)/shard_map/all_gather | solution.py:85
  444.9 6.2 %convolution_subtract_fusion = f32[128,128]{1,0:T(8,128)S(1)} fusion(f32[4096,128]{1,0:T(8,128)S(1)} %fusion.1, f32[128,128]{1,0:T(8,128)S(1)} %copy-done.6, f32[128,128]{1,0:T(8,128)S(1)} %all_gather.18, f32[]{:T(128)S(6)} %pow.7, f32[4096,128]{1,0:T(8,128)} %get-tuple-element.19, f32[]{:T(128)S(6)} %neg.63, f32[]{:T(128)S(6)} %div.173, ...), kind=kOutput, calls=%fused_computation.13 | convolution fusion | flops 809009152 | bytes 6488076 | tf_op jit(solution)/shard_map/dot_general | solution.py:30
  451.2 0.3 fusion.9
  451.5 0.2 fusion.11
  451.7 3.5 fusion.6
  455.2 4.1 fusion.144
  459.4 0.0 all-reduce.10.cloned.1.call-start
  459.4 0.5 all-reduce.10.cloned.1.call-update
  460.0 0.1 broadcast_divide_fusion.2
  460.1 32.0 %reduce-scatter.8.cloned.1.call-done = f32[16,128]{1,0:T(8,128)} async-done(((f32[128,128]{1,0:T(8,128)}), f32[16,128]{1,0:T(8,128)}) %reduce-scatter.8.cloned.1.call-update) | async-done | bytes 8208 | tf_op jit(solution)/shard_map/reduce_scatter | solution.py:89
  492.0 0.8 fusion.64
  492.9 9.2 %all_gather.19 = f32[128,128]{1,0:T(8,128)S(1)} all-gather(f32[16,128]{1,0:T(8,128)S(1)} %fusion.64), channel_id=1, replica_groups=mesh['doc'=4,'feat'=8] {'feat'}, dimensions={0}, use_global_device_ids=true | all-gather | bytes 73728 | tf_op jit(solution)/shard_map/all_gather | solution.py:113
  502.1 45.7 %all-reduce.10.cloned.1.call-done = f32[4096,128]{1,0:T(8,128)} async-done(((f32[4096,128]{1,0:T(8,128)}), f32[4096,128]{1,0:T(8,128)}) %all-reduce.10.cloned.1.call-update) | async-done | bytes 2097168 | tf_op jit(solution)/shard_map/psum | solution.py:93
  547.8 3.2 subtract_multiply_fusion
  551.0 0.6 copy.17
  (38 shorter events, 0.3 us)
Async XLA Ops:
  8.0 162.1 %reduce-scatter.4.cloned.1.call-start = ((), (), s32[]{:S(2)}) async-start(), calls=%async_computation.4 | async-start | bytes 73728 | tf_op jit(solution)/shard_map/reduce_scatter | solution.py:89
  8.0 28.5 %collective-permute-start = (bf16[128,4096]{1,0:T(8,128)(2,1)}, bf16[128,4096]{1,0:T(8,128)(2,1)S(1)}, u32[]{:S(2)}, u32[]{:S(2)}) collective-permute-start(bf16[128,4096]{1,0:T(8,128)(2,1)} %param.11), channel_id=1, source_target_pairs={{0,8},{8,16},{16,24},{24,0},{1,9},{9,17},{17,25},{25,1},{2,10},{10... | collective-permute-start | bytes 3145736 | tf_op jit(solution)/shard_map/ppermute | solution.py:21
  36.5 26.1 %collective-permute-start.1 = (bf16[128,4096]{1,0:T(8,128)(2,1)S(1)}, bf16[128,4096]{1,0:T(8,128)(2,1)S(1)}, u32[]{:S(2)}, u32[]{:S(2)}) collective-permute-start(bf16[128,4096]{1,0:T(8,128)(2,1)S(1)} %collective-permute-done), channel_id=1, source_target_pairs={{0,8},{8,16},{16,24},{24,0},{1,9},{9,17},{17,25},{25,1},{2,10},{10... | collective-permute-start | bytes 3145736 | tf_op jit(solution)/shard_map/ppermute | solution.py:21
  38.7 2.4 copy-start.5
  41.2 30.8 %copy-start.11 = (bf16[128,64]{0,1:T(8,128)(2,1)S(1)}, bf16[128,64]{0,1:T(8,128)(2,1)}, u32[]{:S(2)}) copy-start(bf16[128,64]{0,1:T(8,128)(2,1)} %param.10) | copy-start | bytes 49156
  62.7 25.3 %collective-permute-start.2 = (bf16[128,4096]{1,0:T(8,128)(2,1)S(1)}, bf16[128,4096]{1,0:T(8,128)(2,1)S(1)}, u32[]{:S(2)}, u32[]{:S(2)}) collective-permute-start(bf16[128,4096]{1,0:T(8,128)(2,1)S(1)} %collective-permute-done.1), channel_id=1, source_target_pairs={{0,8},{8,16},{16,24},{24,0},{1,9},{9,17},{17,25},{25,1},{2,10},{10... | collective-permute-start | bytes 3145736 | tf_op jit(solution)/shard_map/ppermute | solution.py:21
  82.1 6.9 %copy-start.8 = (f32[4096]{0:T(1024)S(1)}, f32[4096]{0:T(1024)}, u32[]{:S(2)}) copy-start(f32[4096]{0:T(1024)} %param.12) | copy-start | bytes 49156
  138.6 87.2 %all-reduce.6.cloned.1.call-start = ((), (), s32[]{:S(2)}) async-start(), calls=%async_computation.3 | async-start | bytes 4194304 | tf_op jit(solution)/shard_map/psum | solution.py:93
  139.2 192.0 %reduce-scatter.6.cloned.1.call-start = ((), (), s32[]{:S(2)}) async-start(), calls=%async_computation.6 | async-start | bytes 73728 | tf_op jit(solution)/shard_map/reduce_scatter | solution.py:89
  172.9 99.3 %copy-start.10 = (f32[16,128]{1,0:T(8,128)S(1)}, f32[16,128]{1,0:T(8,128)}, u32[]{:S(2)}) copy-start(f32[16,128]{1,0:T(8,128)} %reduce-scatter.4.cloned.1.call-done) | copy-start | bytes 24580
  172.9 109.9 %copy-start.7 = (f32[128,128]{1,0:T(8,128)S(1)}, f32[128,128]{1,0:T(8,128)}, u32[]{:S(2)}) copy-start(f32[128,128]{1,0:T(8,128)} %fusion.142) | copy-start | bytes 196612
  282.9 6.7 %copy-start = (f32[4096,128]{1,0:T(8,128)S(1)}, f32[4096,128]{1,0:T(8,128)}, u32[]{:S(2)}) copy-start(f32[4096,128]{1,0:T(8,128)} %fusion.141) | copy-start | bytes 6291460
  282.9 6.7 %copy-start.1 = (f32[4096,128]{1,0:T(8,128)S(1)}, f32[4096,128]{1,0:T(8,128)}, u32[]{:S(2)}) copy-start(f32[4096,128]{1,0:T(8,128)} %all-reduce.6.cloned.1.call-done) | copy-start | bytes 6291460
  293.1 1.3 copy-start.2
  298.5 0.7 copy-start.12
  298.5 88.4 %all-reduce.8.cloned.1.call-start = ((), (), s32[]{:S(2)}) async-start(), calls=%async_computation.5 | async-start | bytes 4194304 | tf_op jit(solution)/shard_map/psum | solution.py:93
  299.1 192.9 %reduce-scatter.8.cloned.1.call-start = ((), (), s32[]{:S(2)}) async-start(), calls=%async_computation.7 | async-start | bytes 73728 | tf_op jit(solution)/shard_map/reduce_scatter | solution.py:89
  332.7 101.9 %copy-start.9 = (f32[16,128]{1,0:T(8,128)S(1)}, f32[16,128]{1,0:T(8,128)}, u32[]{:S(2)}) copy-start(f32[16,128]{1,0:T(8,128)} %reduce-scatter.6.cloned.1.call-done) | copy-start | bytes 24580
  332.7 112.2 %copy-start.6 = (f32[128,128]{1,0:T(8,128)S(1)}, f32[128,128]{1,0:T(8,128)}, u32[]{:S(2)}) copy-start(f32[128,128]{1,0:T(8,128)} %fusion.143) | copy-start | bytes 196612
  444.9 6.8 %copy-start.3 = (f32[4096,128]{1,0:T(8,128)S(1)}, f32[4096,128]{1,0:T(8,128)}, u32[]{:S(2)}) copy-start(f32[4096,128]{1,0:T(8,128)} %get-tuple-element.19) | copy-start | bytes 6291460
  444.9 6.8 %copy-start.4 = (f32[4096,128]{1,0:T(8,128)S(1)}, f32[4096,128]{1,0:T(8,128)}, u32[]{:S(2)}) copy-start(f32[4096,128]{1,0:T(8,128)} %all-reduce.8.cloned.1.call-done) | copy-start | bytes 6291460
  459.4 88.4 %all-reduce.10.cloned.1.call-start = ((), (), s32[]{:S(2)}) async-start(), calls=%async_computation.8 | async-start | bytes 4194304 | tf_op jit(solution)/shard_map/psum | solution.py:93
Sparse Core Ops, SparseCore 0:
  138.8 31.2 reduce-scatter.3
  298.6 32.5 reduce-scatter.5
  459.5 32.5 reduce-scatter.7
Sparse Core Ops, SparseCore 1:
  142.1 83.7 all-reduce.5
  302.0 84.9 all-reduce.7
  462.8 84.9 all-reduce.9
